TPU v7x, 1024 devices: a whole 4x4x32 slice. The times are simulated.
1024 devices in a mesh: ctx: 32 (over x, z_lo), fsdp: 32 (over y, z_hi, core).
Axes of the slice: x: 4, y: 4, z: 32 (z_hi: 4, z_lo: 8; z = z_hi * 8 + z_lo), core: 2. Of those that a mesh axis runs over, the one named last changes fastest.
Arguments:
- tokens: bfloat16 [8192, 7168], P('ctx', 'fsdp'), may hold values from -6 to 6
- kv_down: bfloat16 [7168, 576], P('fsdp'), may hold values from -0.0625 to 0.0625
- norm_gain: float32 [512], replicated, may hold values from 0.1 to 1.9
- queries: bfloat16 [8192, 128, 576], P('ctx', 'fsdp'), may hold values from -102 to 102, as said below
Outputs:
- mixed: bfloat16 [8192, 128, 512], P('ctx', 'fsdp')
Inputs may be any that keep to these rules, and one draw needn't show every extreme that they name: real-valued queries.
All inputs are finite; a program needn't handle non-finite values.
Results may differ from a plain program's by a relative error of at most 0.01225.
The roundings to bfloat16 on the way count: a program that leaves them out, or rounds other values in their place, can miss the bound.
Values may be sent and summed in bfloat16 or wider, within the bound.
No kernel may reach another device: no remote copies, remote signals or barrier semaphores. Data moves between devices by JAX's collectives and lax.ppermute only.
A program may use at most 32 MiB of HBM per device.

v0:
```python
import jax
import jax.numpy as jnp
from jax import lax
from jax.sharding import PartitionSpec as P

LATENT = 512
ROPE = 64
REACH = 3


epsilon = 1e-06
theta_base = 10000.0
score_scale = 192.0 ** (-0.5)


def shifted(block, axis, distance):
    devices = range(lax.axis_size(axis))
    route = [(i - distance, i) for i in devices if i - distance in devices]
    return lax.ppermute(block, axis, route)


def finish(kv_raw, norm_gain, first_row):
    row_count = kv_raw.shape[0]
    latent_raw = kv_raw[:, :LATENT]
    squares = jnp.mean(latent_raw * latent_raw, axis=1, keepdims=True)
    latent = latent_raw * lax.rsqrt(squares + epsilon) * norm_gain[None, :]
    half_size = ROPE // 2
    positions = (first_row + jnp.arange(row_count, dtype=jnp.int32)).astype(jnp.float32)
    frequency = theta_base ** (-jnp.arange(half_size, dtype=jnp.float32) / half_size)
    phases = positions[:, None] * frequency[None, :]
    cosine = jnp.cos(phases)
    sine = jnp.sin(phases)
    first_half = kv_raw[:, LATENT : LATENT + half_size]
    second_half = kv_raw[:, LATENT + half_size :]
    rotated = jnp.concatenate(
        [first_half * cosine - second_half * sine, first_half * sine + second_half * cosine], axis=1
    )
    return jnp.concatenate([latent, rotated], axis=1).astype(jnp.bfloat16)


def attend(query_block, window, query_first, key_first):
    query_count = query_block.shape[0]
    key_count = window.shape[0]
    scores = (
        jnp.einsum("thd,kd->thk", query_block, window, preferred_element_type=jnp.float32)
        * score_scale
    )
    query_pos = query_first + jnp.arange(query_count, dtype=jnp.int32)
    key_pos = key_first + jnp.arange(key_count, dtype=jnp.int32)
    allowed = (key_pos[None, :] >= 0) & (key_pos[None, :] <= query_pos[:, None])
    scores = jnp.where(allowed[:, None, :], scores, jnp.float32(-1e30))
    highest = jnp.max(scores, axis=2, keepdims=True)
    expd = jnp.exp(scores - highest)
    weight_sum = jnp.sum(expd, axis=2, keepdims=True)
    weights = expd.astype(jnp.bfloat16)
    mixed = (
        jnp.einsum("thk,kd->thd", weights, window[:, :LATENT], preferred_element_type=jnp.float32)
        / weight_sum
    )
    return mixed.astype(jnp.bfloat16)


def per_device(tokens, kv_down, norm_gain, queries):
    row_count = tokens.shape[0]
    first_row = lax.axis_index("ctx") * row_count
    partial_value = jnp.dot(tokens, kv_down, preferred_element_type=jnp.float32)
    summed = lax.psum(partial_value, "fsdp")
    key_rows = finish(summed, norm_gain, first_row)
    earlier = []
    passing = key_rows
    for distance in range(REACH):
        passing = shifted(passing, "ctx", 1)
        earlier.insert(0, passing)
    window = jnp.concatenate(earlier + [key_rows], axis=0)
    return attend(queries, window, first_row, first_row - REACH * row_count)


def solution(mesh):
    placed = (P("ctx", "fsdp"), P("fsdp", None), P(), P("ctx", "fsdp", None))
    return jax.shard_map(
        per_device, mesh=mesh, in_specs=placed, out_specs=P("ctx", "fsdp", None), check_vma=False
    )
```

profile of v0, /device:TPU:2, one launch (start us, length us, event | category | flops | bytes accessed | tf_op | source)
XLA Modules:
  0.0 577.3 jit_solution(5049115525558690310)
XLA Ops:
  6.5 0.0 copy-start
  6.5 0.0 all-reduce.2.cloned.1.call-start
  6.5 2.2 fusion.24
  8.8 0.0 all-reduce.2.cloned.1.call-update
  8.8 499.2 %all-reduce.2.cloned.1.call-done = f32[256,576]{0,1:T(8,128)} async-done(((f32[256,576]{0,1:T(8,128)}), f32[256,576]{0,1:T(8,128)}) %all-reduce.2.cloned.1.call-update) | async-done | bytes 589840 | tf_op jit(solution)/shard_map/psum | solution.py:67
  508.0 1.1 multiply_reduce_fusion
  509.2 1.0 fusion.18
  510.1 1.2 multiply_convert_fusion
  511.3 3.4 collective-permute-start
  514.8 15.0 %collective-permute-done = bf16[256,576]{0,1:T(8,128)(2,1)S(1)} collective-permute-done((bf16[256,576]{0,1:T(8,128)(2,1)S(1)}, bf16[256,576]{0,1:T(8,128)(2,1)S(1)}, u32[]{:S(2)}, u32[]{:S(2)}) %collective-permute-start) | collective-permute-done | bytes 294944 | tf_op jit(solution)/shard_map/ppermute | solution.py:19
  529.8 1.9 collective-permute-start.1
  531.7 15.6 %collective-permute-done.1 = bf16[256,576]{0,1:T(8,128)(2,1)S(1)} collective-permute-done((bf16[256,576]{0,1:T(8,128)(2,1)S(1)}, bf16[256,576]{0,1:T(8,128)(2,1)S(1)}, u32[]{:S(2)}, u32[]{:S(2)}) %collective-permute-start.1) | collective-permute-done | bytes 294944 | tf_op jit(solution)/shard_map/ppermute | solution.py:19
  547.3 1.9 collective-permute-start.2
  549.3 0.3 compare_and_fusion
  549.6 14.4 %collective-permute-done.2 = bf16[256,576]{0,1:T(8,128)(2,1)S(1)} collective-permute-done((bf16[256,576]{0,1:T(8,128)(2,1)S(1)}, bf16[256,576]{0,1:T(8,128)(2,1)S(1)}, u32[]{:S(2)}, u32[]{:S(2)}) %collective-permute-start.2) | collective-permute-done | bytes 294944 | tf_op jit(solution)/shard_map/ppermute | solution.py:19
  564.0 0.0 copy-done
  564.0 2.1 fusion.2
  566.1 0.9 fusion
  567.0 0.1 maximum_maximum_fusion
  567.2 1.4 divide_convert_fusion
  568.6 1.8 copy.7
  (7 shorter events, 0.1 us)
Async XLA Ops:
  6.5 557.4 %copy-start = (bf16[256,4,576]{0,2,1:T(8,128)(2,1)S(1)}, bf16[256,4,576]{0,2,1:T(8,128)(2,1)}, u32[]{:S(2)}) copy-start(bf16[256,4,576]{0,2,1:T(8,128)(2,1)} %param.7) | copy-start | bytes 3538948
  6.5 501.5 %all-reduce.2.cloned.1.call-start = ((), (), s32[]{:S(2)}) async-start(), calls=%async_computation | async-start | bytes 1179648 | tf_op jit(solution)/shard_map/psum | solution.py:67
  511.3 18.4 %collective-permute-start = (bf16[256,576]{0,1:T(8,128)(2,1)S(1)}, bf16[256,576]{0,1:T(8,128)(2,1)S(1)}, u32[]{:S(2)}, u32[]{:S(2)}) collective-permute-start(bf16[256,576]{0,1:T(8,128)(2,1)S(1)} %pad_maximum_fusion), channel_id=1, source_target_pairs={{0,32},{32,64},{64,96},{96,128},{128,160},{160,192},{192,224},{224... | collective-permute-start | bytes 884744 | tf_op jit(solution)/shard_map/ppermute | solution.py:19
  529.8 17.6 %collective-permute-start.1 = (bf16[256,576]{0,1:T(8,128)(2,1)S(1)}, bf16[256,576]{0,1:T(8,128)(2,1)S(1)}, u32[]{:S(2)}, u32[]{:S(2)}) collective-permute-start(bf16[256,576]{0,1:T(8,128)(2,1)S(1)} %collective-permute-done), channel_id=1, source_target_pairs={{0,32},{32,64},{64,96},{96,128},{128,160},{160,192},{192,224},{224... | collective-permute-start | bytes 884744 | tf_op jit(solution)/shard_map/ppermute | solution.py:19
  547.3 16.6 %collective-permute-start.2 = (bf16[256,576]{0,1:T(8,128)(2,1)S(1)}, bf16[256,576]{0,1:T(8,128)(2,1)S(1)}, u32[]{:S(2)}, u32[]{:S(2)}) collective-permute-start(bf16[256,576]{0,1:T(8,128)(2,1)S(1)} %collective-permute-done.1), channel_id=1, source_target_pairs={{0,32},{32,64},{64,96},{96,128},{128,160},{160,192},{192,224},{224... | collective-permute-start | bytes 884744 | tf_op jit(solution)/shard_map/ppermute | solution.py:19
Sparse Core Ops, SparseCore 0:
  10.9 497.1 all-reduce.1
where the time goes:
time: 578 us; the launch traced here: 577 us
  waiting for transfers between devices  544 us (94%)
  between operations  13.5 us (2%)
  starting transfers between devices  7.26 us (1%)
  matrix products  5.8 us (1%)
    psum x1, waiting for transfers between devices, per_device(): summed = lax.psum(partial_value, 'fsdp')  499 us
    ppermute x3, waiting for transfers between devices, shifted(): return lax.ppermute(block, axis, route)  45 us
  transfers between devices with their start and end apart: 4, of which 4 were waited for; matrix products, arithmetic and copies ran while one was open for 0% of the time, Pallas kernels for 0%

commit v1 on v0

v1 whole, which is shorter than its diff:
```python
import jax
import jax.numpy as jnp
from jax import lax
from jax.sharding import Mesh, PartitionSpec as P

LATENT = 512
ROPE = 64
REACH = 3

X, ZLO, Y, ZHI, CORE = 4, 8, 4, 4, 2
CTX = ("x", "zlo")
FSDP = ("y", "zhi", "core")

epsilon = 1e-06
theta_base = 10000.0
score_scale = 192.0 ** (-0.5)


def finish(kv_raw, norm_gain, positions):
    latent_raw = kv_raw[:, :LATENT]
    squares = jnp.mean(latent_raw * latent_raw, axis=1, keepdims=True)
    latent = latent_raw * lax.rsqrt(squares + epsilon) * norm_gain[None, :]
    half_size = ROPE // 2
    frequency = theta_base ** (-jnp.arange(half_size, dtype=jnp.float32) / half_size)
    phases = positions.astype(jnp.float32)[:, None] * frequency[None, :]
    cosine = jnp.cos(phases)
    sine = jnp.sin(phases)
    first_half = kv_raw[:, LATENT : LATENT + half_size]
    second_half = kv_raw[:, LATENT + half_size :]
    rotated = jnp.concatenate(
        [first_half * cosine - second_half * sine, first_half * sine + second_half * cosine], axis=1
    )
    return jnp.concatenate([latent, rotated], axis=1).astype(jnp.bfloat16)


def attend(query_block, window, query_pos, key_pos):
    scores = (
        jnp.einsum("thd,kd->thk", query_block, window, preferred_element_type=jnp.float32)
        * score_scale
    )
    allowed = (key_pos[None, :] >= 0) & (key_pos[None, :] <= query_pos[:, None])
    scores = jnp.where(allowed[:, None, :], scores, jnp.float32(-1e30))
    highest = jnp.max(scores, axis=2, keepdims=True)
    expd = jnp.exp(scores - highest)
    weight_sum = jnp.sum(expd, axis=2, keepdims=True)
    weights = expd.astype(jnp.bfloat16)
    mixed = (
        jnp.einsum("thk,kd->thd", weights, window[:, :LATENT], preferred_element_type=jnp.float32)
        / weight_sum
    )
    return mixed.astype(jnp.bfloat16)


def earlier_route(distance):
    route = []
    for x in range(X):
        for zlo in range(ZLO):
            for zhi in range(ZHI):
                sx, szlo, szhi = x, zlo - distance, zhi
                if szlo < 0:
                    sx, szlo, szhi = x - 1, szlo + ZLO, (zhi - 1) % ZHI
                if sx >= 0:
                    route.append(((sx * ZLO + szlo) * ZHI + szhi, (x * ZLO + zlo) * ZHI + zhi))
    return route


def per_device(tokens, kv_down, norm_gain, queries):
    row_count = tokens.shape[0]
    width = kv_down.shape[1]
    half = row_count // CORE
    piece = half // Y
    first_row = lax.axis_index(CTX) * row_count
    core = lax.axis_index("core")
    swap = [(0, 1), (1, 0)]

    partial_value = jnp.dot(tokens, kv_down, preferred_element_type=jnp.float32)
    sent = lax.dynamic_slice_in_dim(partial_value, (1 - core) * half, half, 0)
    kept = lax.dynamic_slice_in_dim(partial_value, core * half, half, 0)
    summed = kept + lax.ppermute(sent, "core", swap)
    summed = jnp.sum(lax.all_to_all(summed.reshape(Y, piece, width), "y", 0, 0), axis=0)
    sent = (summed * 64.0).astype(jnp.float16)
    summed = jnp.sum(lax.all_gather(sent, "zhi").astype(jnp.float32), axis=0) * (1.0 / 64.0)

    piece_first = first_row + core * half + lax.axis_index("y") * piece
    key_rows = finish(summed, norm_gain, piece_first + jnp.arange(piece, dtype=jnp.int32))
    blocks = [key_rows] + [
        lax.ppermute(key_rows, ("x", "zlo", "zhi"), earlier_route(d)) for d in range(1, REACH + 1)
    ]
    mine = lax.all_gather(jnp.concatenate(blocks, axis=0), "y", tiled=True)
    other = lax.ppermute(mine, "core", swap)
    window = jnp.concatenate([mine, other], axis=0)

    back = row_count * jnp.arange(REACH + 1, dtype=jnp.int32)
    half_pos = (
        first_row
        + piece * jnp.arange(Y, dtype=jnp.int32)[:, None, None]
        - back[None, :, None]
        + jnp.arange(piece, dtype=jnp.int32)[None, None, :]
    ).reshape(-1)
    key_pos = jnp.concatenate([half_pos + core * half, half_pos + (1 - core) * half])
    query_pos = first_row + jnp.arange(row_count, dtype=jnp.int32)
    return attend(queries, window, query_pos, key_pos)


def solution(mesh):
    fine = Mesh(mesh.devices.reshape(X, ZLO, Y, ZHI, CORE), CTX + FSDP)
    placed = (P(CTX, FSDP), P(FSDP, None), P(), P(CTX, FSDP, None))
    return jax.shard_map(
        per_device, mesh=fine, in_specs=placed, out_specs=P(CTX, FSDP, None), check_vma=False
    )
```

time: 578 us -> 110 us (0.19)
  the two profiles are of different devices: /device:TPU:2 before, /device:TPU:5 now
where the time goes in v1:
time: 110 us
  blocking collectives  54.2 us (49%)
  waiting for transfers between devices  22.8 us (21%)
  starting transfers between devices  22.5 us (20%)
  matrix products  4.99 us (5%)
  local copies, waits for them, and re-layouts  3.15 us (3%)
  other arithmetic  2.17 us (2%)
    all_gather x1, blocking collectives, per_device(): lax.all_gather(sent, 'zhi').astype(jnp.float32)  42.4 us
    ppermute x3, waiting for transfers between devices, per_device(): lax.ppermute(key_rows, ('x', 'zlo', 'zhi'), earlier_route(d))  14.3 us
    all_gather x1, blocking collectives, per_device(): mine = lax.all_gather(jnp.concatenate(blocks, axis=0), 'y', tiled=True)  11.8 us
    ppermute x3, starting transfers between devices, per_device(): lax.ppermute(key_rows, ('x', 'zlo', 'zhi'), earlier_route(d))  9.73 us
    all_to_all x1, waiting for transfers between devices, per_device(): lax.all_to_all(summed.reshape(Y, piece, width), 'y', 0, 0)  6.51 us
    ppermute x1, starting transfers between devices, per_device(): other = lax.ppermute(mine, 'core', swap)  6.05 us
    all_to_all x1, starting transfers between devices, per_device(): lax.all_to_all(summed.reshape(Y, piece, width), 'y', 0, 0)  4.18 us
    ppermute x1, starting transfers between devices, per_device(): summed = kept + lax.ppermute(sent, 'core', swap)  2.58 us
  transfers between devices with their start and end apart: 6, of which 6 were waited for; matrix products, arithmetic and copies ran while one was open for 1% of the time, Pallas kernels for 0%

profile of v1, /device:TPU:5, one launch (start us, length us, event | category | flops | bytes accessed | tf_op | source)
XLA Modules:
  0.0 110.0 jit_solution(2457690271013380032)
XLA Ops:
  0.0 1.4 %fusion.25 = f32[256,576]{0,1:T(8,128)S(1)} fusion(bf16[256,224]{0,1:T(8,128)(2,1)} %param.4, bf16[224,576]{1,0:T(8,128)(2,1)} %param.5), kind=kOutput, calls=%fused_computation.51 | convolution fusion | flops 66060288 | bytes 962560 | tf_op jit(solution)/shard_map/dot_general | solution.py:76
  1.5 2.6 %collective-permute-start = (f32[128,576]{0,1:T(8,128)S(1)}, f32[128,576]{0,1:T(8,128)S(1)}, u32[]{:S(2)}, u32[]{:S(2)}) collective-permute-start(f32[128,576]{0,1:T(8,128)S(1)} %constant_dynamic-slice_fusion), channel_id=1, source_target_pairs={{0,1},{1,0},{2,3},{3,2},{4,5},{5,4},{6,7},{7,6},{8,9},{9,8},{10,11... | collective-permute-start | bytes 884744 | tf_op jit(solution)/shard_map/ppermute | solution.py:79
  4.1 0.1 broadcast_subtract_fusion
  4.2 0.1 fusion.21
  4.3 0.1 add.115
  4.3 0.1 add.112
  4.4 0.8 collective-permute-done
  5.3 0.9 copy.20
  6.2 4.2 %all-to-all-start = ((f32[4,32,576]{2,1,0:T(8,128)}), f32[4,32,576]{2,1,0:T(8,128)S(1)}, u32[]{:S(2)}, u32[]{:S(2)}) async-start(f32[4,32,576]{2,1,0:T(8,128)} %bitcast), calls=%async_computation | async-start | bytes 655360 | tf_op jit(solution)/shard_map/all_to_all | solution.py:80
  10.4 6.5 %all-to-all-done = f32[4,32,576]{2,1,0:T(8,128)S(1)} async-done(((f32[4,32,576]{2,1,0:T(8,128)}), f32[4,32,576]{2,1,0:T(8,128)S(1)}, u32[]{:S(2)}, u32[]{:S(2)}) %all-to-all-start) | async-done | bytes 294944 | tf_op jit(solution)/shard_map/all_to_all | solution.py:80
  16.9 42.4 %all-gather = f16[128,576]{1,0:T(8,128)(2,1)S(1)} all-gather(f16[32,576]{1,0:T(8,128)(2,1)S(1)} %multiply_convert_fusion), channel_id=2, replica_groups=mesh['x'=4,'zlo'=8,'y'=4,'zhi'=4,'core'=2] {'zhi'}, dimensions={0}, use_global_device_ids=true | all-gather | bytes 184320 | tf_op jit(solution)/shard_map/all_gather | solution.py:82
  59.4 0.1 multiply_reduce_fusion
  59.5 0.1 fusion.18
  59.7 0.1 multiply_convert_fusion.1
  59.7 0.1 pad_maximum_fusion.1
  59.8 0.1 copy.24
  60.0 2.9 %collective-permute-start.3 = (bf16[32,576]{0,1:T(8,128)(2,1)S(1)}, bf16[32,576]{0,1:T(8,128)(2,1)S(1)}, u32[]{:S(2)}, u32[]{:S(2)}) collective-permute-start(bf16[32,576]{0,1:T(8,128)(2,1)S(1)} %copy.24), channel_id=1, source_target_pairs={{0,96},{2,98},{4,100},{6,102},{32,128},{34,130},{36,132},{38,134},... | collective-permute-start | bytes 110600 | tf_op jit(solution)/shard_map/ppermute | solution.py:87
  62.8 4.4 %collective-permute-start.2 = (bf16[32,576]{0,1:T(8,128)(2,1)S(1)}, bf16[32,576]{0,1:T(8,128)(2,1)S(1)}, u32[]{:S(2)}, u32[]{:S(2)}) collective-permute-start(bf16[32,576]{0,1:T(8,128)(2,1)S(1)} %copy.24), channel_id=1, source_target_pairs={{0,64},{2,66},{4,68},{6,70},{32,96},{34,98},{36,100},{38,102},{64,... | collective-permute-start | bytes 110600 | tf_op jit(solution)/shard_map/ppermute | solution.py:87
  67.3 2.4 %collective-permute-start.1 = (bf16[32,576]{0,1:T(8,128)(2,1)S(1)}, bf16[32,576]{0,1:T(8,128)(2,1)S(1)}, u32[]{:S(2)}, u32[]{:S(2)}) collective-permute-start(bf16[32,576]{0,1:T(8,128)(2,1)S(1)} %copy.24), channel_id=1, source_target_pairs={{0,32},{2,34},{4,36},{6,38},{32,64},{34,66},{36,68},{38,70},{64,96... | collective-permute-start | bytes 110600 | tf_op jit(solution)/shard_map/ppermute | solution.py:87
  69.7 2.8 %collective-permute-done.3 = bf16[32,576]{0,1:T(8,128)(2,1)S(1)} collective-permute-done((bf16[32,576]{0,1:T(8,128)(2,1)S(1)}, bf16[32,576]{0,1:T(8,128)(2,1)S(1)}, u32[]{:S(2)}, u32[]{:S(2)}) %collective-permute-start.3) | collective-permute-done | bytes 36896 | tf_op jit(solution)/shard_map/ppermute | solution.py:87
  72.5 8.6 %collective-permute-done.2 = bf16[32,576]{0,1:T(8,128)(2,1)S(1)} collective-permute-done((bf16[32,576]{0,1:T(8,128)(2,1)S(1)}, bf16[32,576]{0,1:T(8,128)(2,1)S(1)}, u32[]{:S(2)}, u32[]{:S(2)}) %collective-permute-start.2) | collective-permute-done | bytes 36896 | tf_op jit(solution)/shard_map/ppermute | solution.py:87
  81.1 2.9 %collective-permute-done.1 = bf16[32,576]{0,1:T(8,128)(2,1)S(1)} collective-permute-done((bf16[32,576]{0,1:T(8,128)(2,1)S(1)}, bf16[32,576]{0,1:T(8,128)(2,1)S(1)}, u32[]{:S(2)}, u32[]{:S(2)}) %collective-permute-start.1) | collective-permute-done | bytes 36896 | tf_op jit(solution)/shard_map/ppermute | solution.py:87
  84.0 0.2 pad_maximum_fusion
  84.2 11.8 %all_gather.8 = bf16[512,576]{0,1:T(8,128)(2,1)S(1)} all-gather(bf16[128,576]{0,1:T(8,128)(2,1)S(1)} %pad_maximum_fusion), channel_id=1, replica_groups=mesh['x'=4,'zlo'=8,'y'=4,'zhi'=4,'core'=2] {'y'}, dimensions={0}, use_global_device_ids=true | all-gather | bytes 737280 | tf_op jit(solution)/shard_map/all_gather | solution.py:89
  96.0 6.1 %collective-permute-start.4 = (bf16[512,576]{0,1:T(8,128)(2,1)S(1)}, bf16[512,576]{0,1:T(8,128)(2,1)S(1)}, u32[]{:S(2)}, u32[]{:S(2)}) collective-permute-start(bf16[512,576]{0,1:T(8,128)(2,1)S(1)} %all_gather.8), channel_id=1, source_target_pairs={{0,1},{1,0},{2,3},{3,2},{4,5},{5,4},{6,7},{7,6},{8,9},{9,8},{10,11... | collective-permute-start | bytes 1769480 | tf_op jit(solution)/shard_map/ppermute | solution.py:90
  102.1 0.3 compare_and_fusion
  102.4 0.1 constant_dynamic-update-slice_fusion.2
  102.5 1.2 %collective-permute-done.4 = bf16[512,576]{0,1:T(8,128)(2,1)S(1)} collective-permute-done((bf16[512,576]{0,1:T(8,128)(2,1)S(1)}, bf16[512,576]{0,1:T(8,128)(2,1)S(1)}, u32[]{:S(2)}, u32[]{:S(2)}) %collective-permute-start.4) | collective-permute-done | bytes 589856 | tf_op jit(solution)/shard_map/ppermute | solution.py:90
  103.7 2.2 %fusion.2 = (f32[256,4]{0,1:T(4,128)S(1)}, f32[1024,256,4]{1,0,2:T(8,128)S(1)}) fusion(pred[256,1024]{0,1:T(8,128)(4,1)S(1)} %compare_and_fusion, bf16[256,4,576]{0,2,1:T(8,128)(2,1)S(1)} %copy-done, bf16[1024,576]{0,1:T(8,128)(2,1)S(1)} %constant_dynamic-update-slice_fusion.1), kind=kOutput, calls=%fused_computation.4 | convolution fusion | flops 1211104256 | bytes 6819840 | tf_op jit(solution)/shard_map/thd,kd->thk/dot_general | solution.py:38
  105.9 0.9 fusion
  106.8 1.4 %divide_convert_fusion = bf16[256,4,512]{2,0,1:T(8,128)(2,1)S(1)} fusion(f32[256,4]{0,1:T(4,128)S(1)} %fusion, bf16[1024,576]{0,1:T(8,128)(2,1)S(1)} %constant_dynamic-update-slice_fusion.1, f32[1024,256,4]{1,0,2:T(8,128)S(1)} %get-tuple-element.10, f32[256,4]{0,1:T(4,128)S(1)} %get-tuple-element.9, pred[256,1024]{0,1:T(8,128)(4,1)S(1)} %compare_and_fusion), kind=kOutput, calls=%fused_computation.6 | convolution fusion | flops 1078984704 | bytes 6561792 | tf_op jit(solution)/shard_map/thk,kd->thd/dot_general | solution.py:48
  108.2 1.8 %copy.27 = bf16[256,4,512]{2,1,0:T(4,128)(2,1)} copy(bf16[256,4,512]{2,0,1:T(8,128)(2,1)S(1)} %divide_convert_fusion) | data formatting | bytes 2097152 | tf_op jit(solution)/shard_map/convert_element_type | solution.py:51
  (21 shorter events, 0.3 us)
Async XLA Ops:
  0.0 103.7 %copy-start = (bf16[256,4,576]{0,2,1:T(8,128)(2,1)S(1)}, bf16[256,4,576]{0,2,1:T(8,128)(2,1)}, u32[]{:S(2)}) copy-start(bf16[256,4,576]{0,2,1:T(8,128)(2,1)} %param.7) | copy-start | bytes 3538948
  0.0 59.6 %copy-start.1 = (f32[512]{0:T(512)S(1)}, f32[512]{0:T(512)}, u32[]{:S(2)}) copy-start(f32[512]{0:T(512)} %param.6) | copy-start | bytes 6148
  1.5 3.8 %collective-permute-start = (f32[128,576]{0,1:T(8,128)S(1)}, f32[128,576]{0,1:T(8,128)S(1)}, u32[]{:S(2)}, u32[]{:S(2)}) collective-permute-start(f32[128,576]{0,1:T(8,128)S(1)} %constant_dynamic-slice_fusion), channel_id=1, source_target_pairs={{0,1},{1,0},{2,3},{3,2},{4,5},{5,4},{6,7},{7,6},{8,9},{9,8},{10,11... | collective-permute-start | bytes 884744 | tf_op jit(solution)/shard_map/ppermute | solution.py:79
  6.2 10.7 %all-to-all-start = ((f32[4,32,576]{2,1,0:T(8,128)}), f32[4,32,576]{2,1,0:T(8,128)S(1)}, u32[]{:S(2)}, u32[]{:S(2)}) async-start(f32[4,32,576]{2,1,0:T(8,128)} %bitcast), calls=%async_computation | async-start | bytes 655360 | tf_op jit(solution)/shard_map/all_to_all | solution.py:80
  60.0 12.5 %collective-permute-start.3 = (bf16[32,576]{0,1:T(8,128)(2,1)S(1)}, bf16[32,576]{0,1:T(8,128)(2,1)S(1)}, u32[]{:S(2)}, u32[]{:S(2)}) collective-permute-start(bf16[32,576]{0,1:T(8,128)(2,1)S(1)} %copy.24), channel_id=1, source_target_pairs={{0,96},{2,98},{4,100},{6,102},{32,128},{34,130},{36,132},{38,134},... | collective-permute-start | bytes 110600 | tf_op jit(solution)/shard_map/ppermute | solution.py:87
  62.8 18.3 %collective-permute-start.2 = (bf16[32,576]{0,1:T(8,128)(2,1)S(1)}, bf16[32,576]{0,1:T(8,128)(2,1)S(1)}, u32[]{:S(2)}, u32[]{:S(2)}) collective-permute-start(bf16[32,576]{0,1:T(8,128)(2,1)S(1)} %copy.24), channel_id=1, source_target_pairs={{0,64},{2,66},{4,68},{6,70},{32,96},{34,98},{36,100},{38,102},{64,... | collective-permute-start | bytes 110600 | tf_op jit(solution)/shard_map/ppermute | solution.py:87
  67.3 16.7 %collective-permute-start.1 = (bf16[32,576]{0,1:T(8,128)(2,1)S(1)}, bf16[32,576]{0,1:T(8,128)(2,1)S(1)}, u32[]{:S(2)}, u32[]{:S(2)}) collective-permute-start(bf16[32,576]{0,1:T(8,128)(2,1)S(1)} %copy.24), channel_id=1, source_target_pairs={{0,32},{2,34},{4,36},{6,38},{32,64},{34,66},{36,68},{38,70},{64,96... | collective-permute-start | bytes 110600 | tf_op jit(solution)/shard_map/ppermute | solution.py:87
  96.0 7.7 %collective-permute-start.4 = (bf16[512,576]{0,1:T(8,128)(2,1)S(1)}, bf16[512,576]{0,1:T(8,128)(2,1)S(1)}, u32[]{:S(2)}, u32[]{:S(2)}) collective-permute-start(bf16[512,576]{0,1:T(8,128)(2,1)S(1)} %all_gather.8), channel_id=1, source_target_pairs={{0,1},{1,0},{2,3},{3,2},{4,5},{5,4},{6,7},{7,6},{8,9},{9,8},{10,11... | collective-permute-start | bytes 1769480 | tf_op jit(solution)/shard_map/ppermute | solution.py:90

commit v2 on v1

v2 whole, which is shorter than its diff:
```python
import jax
import jax.numpy as jnp
from jax import lax
from jax.experimental import pallas as pl
from jax.experimental.layout import Layout, with_layout_constraint
from jax.experimental.pallas import tpu as pltpu
from jax.sharding import Mesh, PartitionSpec as P

LATENT = 512
ROPE = 64
REACH = 3

X, ZLO, Y, ZHI, CORE = 4, 8, 4, 4, 2
CTX = ("x", "zlo")
FSDP = ("y", "zhi", "core")

epsilon = 1e-06
theta_base = 10000.0
score_scale = 192.0 ** (-0.5)
LOG2_E = 1.4426950408889634
CHUNKS = 2
HEADS_DEV = 4


def finish(kv_raw, norm_gain, positions):
    latent_raw = kv_raw[:, :LATENT]
    squares = jnp.mean(latent_raw * latent_raw, axis=1, keepdims=True)
    latent = latent_raw * lax.rsqrt(squares + epsilon) * norm_gain[None, :]
    half_size = ROPE // 2
    frequency = theta_base ** (-jnp.arange(half_size, dtype=jnp.float32) / half_size)
    phases = positions.astype(jnp.float32)[:, None] * frequency[None, :]
    cosine = jnp.cos(phases)
    sine = jnp.sin(phases)
    first_half = kv_raw[:, LATENT : LATENT + half_size]
    second_half = kv_raw[:, LATENT + half_size :]
    rotated = jnp.concatenate(
        [first_half * cosine - second_half * sine, first_half * sine + second_half * cosine], axis=1
    )
    return jnp.concatenate([latent, rotated], axis=1).astype(jnp.bfloat16)


def attend_kernel(place_ref, q_ref, mine_ref, other_ref, out_ref):
    heads = out_ref.shape[1]
    rows = q_ref.shape[0] // CHUNKS
    keys = mine_ref.shape[0] * mine_ref.shape[2]
    first_row, core = place_ref[0], place_ref[1]
    piece = keys // (Y * (REACH + 1))
    block = piece * Y * CORE
    key = lax.broadcasted_iota(jnp.int32, (1, keys), 1)
    local = (
        key // (piece * (REACH + 1)) * piece
        + key % piece
        - key // piece % (REACH + 1) * block
    )
    bounds = []
    for half in (core, 1 - core):
        from_first = local + half * (piece * Y)
        bounds.append(jnp.where(from_first < -first_row, 1 << 20, from_first))
    halves = [
        jnp.concatenate([ref[y] for y in range(Y)], axis=1) for ref in (mine_ref, other_ref)
    ]

    def products(n):
        q = q_ref[n * rows : (n + 1) * rows, :]
        return [jnp.dot(q, half, preferred_element_type=jnp.float32) for half in halves]

    ahead = products(0)
    for n in range(CHUNKS):
        now = ahead
        if n + 1 < CHUNKS:
            ahead = products(n + 1)
        token = (lax.broadcasted_iota(jnp.int32, (rows, 1), 0) + n * rows) // heads
        now = [jnp.where(bound <= token, v, -1e30) for v, bound in zip(now, bounds)]
        highest = jnp.maximum(*[jnp.max(v, axis=1, keepdims=True) for v in now])
        expd = [jnp.exp2((v - highest) * (score_scale * LOG2_E)) for v in now]
        weight_sum = sum(jnp.sum(v, axis=1, keepdims=True) for v in expd)
        mixed = sum(
            lax.dot_general(
                v.astype(jnp.bfloat16),
                half[:LATENT],
                (((1,), (1,)), ((), ())),
                preferred_element_type=jnp.float32,
            )
            for v, half in zip(expd, halves)
        )
        mixed = mixed * (1.0 / weight_sum)
        out_ref[n * rows // heads : (n + 1) * rows // heads] = mixed.reshape(
            rows // heads, heads, LATENT
        ).astype(jnp.bfloat16)


def attend(query_rows, mine, other, first_row, core):
    whole = pl.BlockSpec(memory_space=pltpu.VMEM)
    rows = query_rows.shape[0]
    return pl.pallas_call(
        attend_kernel,
        out_shape=jax.ShapeDtypeStruct((rows // HEADS_DEV, HEADS_DEV, LATENT), jnp.bfloat16),
        in_specs=[pl.BlockSpec(memory_space=pltpu.SMEM), whole, whole, whole],
        out_specs=whole,
        name="attend",
        compiler_params=pltpu.CompilerParams(vmem_limit_bytes=40 << 20),
    )(
        jnp.stack([first_row, core]).astype(jnp.int32),
        query_rows,
        mine,
        other,
    )


def earlier_route(distance):
    route = []
    for x in range(X):
        for zlo in range(ZLO):
            for zhi in range(ZHI):
                sx, szlo, szhi = x, zlo - distance, zhi
                if szlo < 0:
                    sx, szlo, szhi = x - 1, szlo + ZLO, (zhi - 1) % ZHI
                if sx >= 0:
                    route.append(((sx * ZLO + szlo) * ZHI + szhi, (x * ZLO + zlo) * ZHI + zhi))
    return route


def per_device(tokens, kv_down, norm_gain, queries):
    row_count = tokens.shape[0]
    width = kv_down.shape[1]
    half = row_count // CORE
    piece = half // Y
    first_row = lax.axis_index(CTX) * row_count
    core = lax.axis_index("core")
    swap = [(0, 1), (1, 0)]

    partial_value = jnp.dot(tokens, kv_down, preferred_element_type=jnp.float32)
    partial_value = with_layout_constraint(partial_value, Layout((0, 1)))
    sent = lax.dynamic_slice_in_dim(partial_value, (1 - core) * half, half, 0)
    kept = lax.dynamic_slice_in_dim(partial_value, core * half, half, 0)
    summed = kept + lax.ppermute(sent, "core", swap)
    summed, queries = lax.optimization_barrier((summed, queries))
    summed = lax.all_to_all(summed.reshape(Y, piece, width), "y", 0, 0)
    summed, query_rows = lax.optimization_barrier((summed, queries.reshape(-1, width)))
    summed = jnp.sum(summed, axis=0)
    sent = (summed * 64.0).astype(jnp.float16)
    summed = jnp.sum(lax.all_gather(sent, "zhi").astype(jnp.float32), axis=0) * (1.0 / 64.0)

    piece_first = first_row + core * half + lax.axis_index("y") * piece
    key_rows = finish(summed, norm_gain, piece_first + jnp.arange(piece, dtype=jnp.int32))
    pair = jnp.concatenate(
        [key_rows, lax.ppermute(key_rows, ("x", "zlo", "zhi"), earlier_route(1))], axis=0
    )
    pieces = jnp.concatenate(
        [pair, lax.ppermute(pair, ("x", "zlo", "zhi"), earlier_route(2))], axis=0
    )
    keys = pieces.T
    mine = lax.all_to_all(jnp.broadcast_to(keys[None], (Y,) + keys.shape), "y", 0, 0)
    other = lax.ppermute(mine, "core", swap)
    return attend(query_rows, mine, other, first_row, core)


def solution(mesh):
    fine = Mesh(mesh.devices.reshape(X, ZLO, Y, ZHI, CORE), CTX + FSDP)
    placed = (P(CTX, FSDP), P(FSDP, None), P(), P(CTX, FSDP, None))
    return jax.shard_map(
        per_device, mesh=fine, in_specs=placed, out_specs=P(CTX, FSDP, None), check_vma=False
    )
```

time: 110 us -> 103 us (0.936)
  the two profiles are of different devices: /device:TPU:5 before, /device:TPU:2 now
where the time goes in v2:
time: 103 us; the launch traced here: 102 us
  blocking collectives  56.5 us (55%)
  waiting for transfers between devices  19.8 us (19%)
  starting transfers between devices  13.4 us (13%)
  local copies, waits for them, and re-layouts  4.71 us (5%)
  Pallas kernels  4.69 us (5%)
  other arithmetic  1.5 us (1%)
  matrix products  1.19 us (1%)
    all_gather x1, blocking collectives, per_device(): lax.all_gather(sent, 'zhi').astype(jnp.float32)  45.7 us
    all_to_all x1, blocking collectives, per_device(): lax.all_to_all(jnp.broadcast_to(keys[None], (Y,) + keys.shape), 'y', 0, 0)  10.8 us
    ppermute x1, waiting for transfers between devices, per_device(): lax.ppermute(pair, ('x', 'zlo', 'zhi'), earlier_route(2))  7.41 us
    ppermute x1, waiting for transfers between devices, per_device(): lax.ppermute(key_rows, ('x', 'zlo', 'zhi'), earlier_route(1))  4.77 us
    pallas_call x1, Pallas kernels, attend(): pl.pallas_call(attend_kernel, out_shape=jax.ShapeDtypeStruct((rows // HEA...  4.69 us
    all_to_all x1, starting transfers between devices, per_device(): summed = lax.all_to_all(summed.reshape(Y, piece, width), 'y', 0, 0)  4.46 us
    all_to_all x1, waiting for transfers between devices, per_device(): summed = lax.all_to_all(summed.reshape(Y, piece, width), 'y', 0, 0)  4.13 us
    ppermute x1, starting transfers between devices, per_device(): lax.ppermute(key_rows, ('x', 'zlo', 'zhi'), earlier_route(1))  3.22 us
  transfers between devices with their start and end apart: 5, of which 5 were waited for; matrix products, arithmetic and copies ran while one was open for 4% of the time, Pallas kernels for 0%

profile of v2, /device:TPU:2, one launch (start us, length us, event | category | flops | bytes accessed | tf_op | source)
XLA Modules:
  0.0 101.9 jit_solution(8328608165322739500)
XLA Ops:
  0.0 0.0 copy-start
  0.0 1.0 copy-done
  1.0 1.2 %fusion.8 = f32[256,576]{1,0:T(8,128)S(1)} fusion(bf16[256,224]{0,1:T(8,128)(2,1)} %param.4, bf16[224,576]{1,0:T(8,128)(2,1)S(1)} %copy-done), kind=kOutput, calls=%fused_computation.24 | convolution fusion | flops 66060288 | bytes 962560 | tf_op jit(solution)/shard_map/dot_general | solution.py:132
  2.2 1.9 %collective-permute-start = (f32[128,576]{1,0:T(8,128)S(1)}, f32[128,576]{1,0:T(8,128)S(1)}, u32[]{:S(2)}, u32[]{:S(2)}) collective-permute-start(f32[128,576]{1,0:T(8,128)S(1)} %constant_dynamic-slice_fusion), channel_id=1, source_target_pairs={{0,1},{1,0},{2,3},{3,2},{4,5},{5,4},{6,7},{7,6},{8,9},{9,8},{10,11... | collective-permute-start | bytes 884744 | tf_op jit(solution)/shard_map/ppermute | solution.py:136
  4.1 1.6 %collective-permute-done = f32[128,576]{1,0:T(8,128)S(1)} collective-permute-done((f32[128,576]{1,0:T(8,128)S(1)}, f32[128,576]{1,0:T(8,128)S(1)}, u32[]{:S(2)}, u32[]{:S(2)}) %collective-permute-start) | collective-permute-done | bytes 294944 | tf_op jit(solution)/shard_map/ppermute | solution.py:136
  5.7 0.8 dynamic-slice_add_fusion
  6.5 4.5 %all-to-all-start = ((f32[4,32,576]{2,1,0:T(8,128)}), f32[4,32,576]{2,1,0:T(8,128)S(1)}, u32[]{:S(2)}, u32[]{:S(2)}) async-start(f32[4,32,576]{2,1,0:T(8,128)} %bitcast.2), calls=%async_computation | async-start | bytes 655360 | tf_op jit(solution)/shard_map/all_to_all | solution.py:138
  11.0 2.8 %copy.9 = bf16[256,4,576]{2,1,0:T(4,128)(2,1)S(1)} copy(bf16[256,4,576]{0,2,1:T(8,128)(2,1)} %param.7) | data formatting | bytes 2359296 | tf_op jit(solution)/shard_map/optimization_barrier | solution.py:137
  13.8 0.0 copy-start.1
  13.8 0.7 reshape.41.q_ref
  14.5 4.1 %all-to-all-done = f32[4,32,576]{2,1,0:T(8,128)S(1)} async-done(((f32[4,32,576]{2,1,0:T(8,128)}), f32[4,32,576]{2,1,0:T(8,128)S(1)}, u32[]{:S(2)}, u32[]{:S(2)}) %all-to-all-start) | async-done | bytes 294944 | tf_op jit(solution)/shard_map/all_to_all | solution.py:138
  18.7 45.7 %all-gather = f16[128,576]{1,0:T(8,128)(2,1)S(1)} all-gather(f16[32,576]{1,0:T(8,128)(2,1)S(1)} %multiply_convert_fusion), channel_id=2, replica_groups=mesh['x'=4,'zlo'=8,'y'=4,'zhi'=4,'core'=2] {'zhi'}, dimensions={0}, use_global_device_ids=true | all-gather | bytes 184320 | tf_op jit(solution)/shard_map/all_gather | solution.py:142
  64.4 0.1 multiply_reduce_fusion
  64.5 0.1 fusion.5
  64.6 0.0 copy-done.1
  64.7 0.1 multiply_convert_fusion.1
  64.7 0.1 pad_maximum_fusion.1
  64.8 3.2 %collective-permute-start.1 = (bf16[32,576]{1,0:T(8,128)(2,1)S(1)}, bf16[32,576]{1,0:T(8,128)(2,1)S(1)}, u32[]{:S(2)}, u32[]{:S(2)}) collective-permute-start(bf16[32,576]{1,0:T(8,128)(2,1)S(1)} %pad_maximum_fusion.1), channel_id=1, source_target_pairs={{0,32},{2,34},{4,36},{6,38},{32,64},{34,66},{36,68},{38,70},{64,96... | collective-permute-start | bytes 110600 | tf_op jit(solution)/shard_map/ppermute | solution.py:147
  68.0 4.8 %collective-permute-done.1 = bf16[32,576]{1,0:T(8,128)(2,1)S(1)} collective-permute-done((bf16[32,576]{1,0:T(8,128)(2,1)S(1)}, bf16[32,576]{1,0:T(8,128)(2,1)S(1)}, u32[]{:S(2)}, u32[]{:S(2)}) %collective-permute-start.1) | collective-permute-done | bytes 36896 | tf_op jit(solution)/shard_map/ppermute | solution.py:147
  72.8 0.1 pad_maximum_fusion
  72.9 1.9 %collective-permute-start.2 = (bf16[64,576]{1,0:T(8,128)(2,1)S(1)}, bf16[64,576]{1,0:T(8,128)(2,1)S(1)}, u32[]{:S(2)}, u32[]{:S(2)}) collective-permute-start(bf16[64,576]{1,0:T(8,128)(2,1)S(1)} %pad_maximum_fusion), channel_id=1, source_target_pairs={{0,64},{2,66},{4,68},{6,70},{32,96},{34,98},{36,100},{38,102},{64,... | collective-permute-start | bytes 221192 | tf_op jit(solution)/shard_map/ppermute | solution.py:150
  74.8 7.4 %collective-permute-done.2 = bf16[64,576]{1,0:T(8,128)(2,1)S(1)} collective-permute-done((bf16[64,576]{1,0:T(8,128)(2,1)S(1)}, bf16[64,576]{1,0:T(8,128)(2,1)S(1)}, u32[]{:S(2)}, u32[]{:S(2)}) %collective-permute-start.2) | collective-permute-done | bytes 73760 | tf_op jit(solution)/shard_map/ppermute | solution.py:150
  82.2 0.1 maximum_bitcast_fusion
  82.3 0.1 copy.10
  82.4 0.1 broadcast_in_dim.2
  82.5 10.8 %all_to_all.10.mine_ref = bf16[4,576,128]{2,1,0:T(8,128)(2,1)S(1)} all-to-all(bf16[4,576,128]{2,1,0:T(8,128)(2,1)S(1)} %broadcast_in_dim.2), channel_id=1, replica_groups=mesh['x'=4,'zlo'=8,'y'=4,'zhi'=4,'core'=2] {'y'}, dimensions={0} | all-to-all | bytes 1179648 | tf_op jit(solution)/shard_map/all_to_all | solution.py:153
  93.4 1.9 %collective-permute-start.3 = (bf16[4,576,128]{2,1,0:T(8,128)(2,1)S(1)}, bf16[4,576,128]{2,1,0:T(8,128)(2,1)S(1)}, u32[]{:S(2)}, u32[]{:S(2)}) collective-permute-start(bf16[4,576,128]{2,1,0:T(8,128)(2,1)S(1)} %all_to_all.10.mine_ref), channel_id=1, source_target_pairs={{0,1},{1,0},{2,3},{3,2},{4,5},{5,4},{6,7},{7,6},{8,9},{9,8},{10,11... | collective-permute-start | bytes 1769480 | tf_op jit(solution)/shard_map/ppermute | solution.py:154
  95.3 0.1 pad_add_fusion.place_ref
  95.4 1.9 %collective-permute-done.3.other_ref = bf16[4,576,128]{2,1,0:T(8,128)(2,1)S(1)} collective-permute-done((bf16[4,576,128]{2,1,0:T(8,128)(2,1)S(1)}, bf16[4,576,128]{2,1,0:T(8,128)(2,1)S(1)}, u32[]{:S(2)}, u32[]{:S(2)}) %collective-permute-start.3) | collective-permute-done | bytes 589856 | tf_op jit(solution)/shard_map/ppermute | solution.py:154
  97.2 4.7 %attend.1 = bf16[256,4,512]{2,1,0:T(4,128)(2,1)} custom-call(s32[2]{0:T(128)S(1)} %pad_add_fusion.place_ref, bf16[1024,576]{1,0:T(8,128)(2,1)S(1)} %reshape.41.q_ref, bf16[4,576,128]{2,1,0:T(8,128)(2,1)S(1)} %all_to_all.10.mine_ref, bf16[4,576,128]{2,1,0:T(8,128)(2,1)S(1)} %collective-permute-done.3.other_ref), custom_call_target="tpu_custom_call" | custom-call | tf_op jit(solution)/shard_map/attend/pallas_call | solution.py:95
  (8 shorter events, 0.1 us)
Async XLA Ops:
  0.0 1.0 copy-start
  2.2 3.5 %collective-permute-start = (f32[128,576]{1,0:T(8,128)S(1)}, f32[128,576]{1,0:T(8,128)S(1)}, u32[]{:S(2)}, u32[]{:S(2)}) collective-permute-start(f32[128,576]{1,0:T(8,128)S(1)} %constant_dynamic-slice_fusion), channel_id=1, source_target_pairs={{0,1},{1,0},{2,3},{3,2},{4,5},{5,4},{6,7},{7,6},{8,9},{9,8},{10,11... | collective-permute-start | bytes 884744 | tf_op jit(solution)/shard_map/ppermute | solution.py:136
  6.5 12.1 %all-to-all-start = ((f32[4,32,576]{2,1,0:T(8,128)}), f32[4,32,576]{2,1,0:T(8,128)S(1)}, u32[]{:S(2)}, u32[]{:S(2)}) async-start(f32[4,32,576]{2,1,0:T(8,128)} %bitcast.2), calls=%async_computation | async-start | bytes 655360 | tf_op jit(solution)/shard_map/all_to_all | solution.py:138
  13.8 50.9 %copy-start.1 = (f32[512]{0:T(512)S(1)}, f32[512]{0:T(512)}, u32[]{:S(2)}) copy-start(f32[512]{0:T(512)} %param.6) | copy-start | bytes 6148
  64.8 8.0 %collective-permute-start.1 = (bf16[32,576]{1,0:T(8,128)(2,1)S(1)}, bf16[32,576]{1,0:T(8,128)(2,1)S(1)}, u32[]{:S(2)}, u32[]{:S(2)}) collective-permute-start(bf16[32,576]{1,0:T(8,128)(2,1)S(1)} %pad_maximum_fusion.1), channel_id=1, source_target_pairs={{0,32},{2,34},{4,36},{6,38},{32,64},{34,66},{36,68},{38,70},{64,96... | collective-permute-start | bytes 110600 | tf_op jit(solution)/shard_map/ppermute | solution.py:147
  72.9 9.3 %collective-permute-start.2 = (bf16[64,576]{1,0:T(8,128)(2,1)S(1)}, bf16[64,576]{1,0:T(8,128)(2,1)S(1)}, u32[]{:S(2)}, u32[]{:S(2)}) collective-permute-start(bf16[64,576]{1,0:T(8,128)(2,1)S(1)} %pad_maximum_fusion), channel_id=1, source_target_pairs={{0,64},{2,66},{4,68},{6,70},{32,96},{34,98},{36,100},{38,102},{64,... | collective-permute-start | bytes 221192 | tf_op jit(solution)/shard_map/ppermute | solution.py:150
  93.4 3.9 %collective-permute-start.3 = (bf16[4,576,128]{2,1,0:T(8,128)(2,1)S(1)}, bf16[4,576,128]{2,1,0:T(8,128)(2,1)S(1)}, u32[]{:S(2)}, u32[]{:S(2)}) collective-permute-start(bf16[4,576,128]{2,1,0:T(8,128)(2,1)S(1)} %all_to_all.10.mine_ref), channel_id=1, source_target_pairs={{0,1},{1,0},{2,3},{3,2},{4,5},{5,4},{6,7},{7,6},{8,9},{9,8},{10,11... | collective-permute-start | bytes 1769480 | tf_op jit(solution)/shard_map/ppermute | solution.py:154
